TPU v7x, 32 devices: a whole 2x2x4 slice. The times are simulated.
32 devices in a mesh: grp: 4 (over x, core), tbl: 8 (over z, y).
Axes of the slice: x: 2, y: 2, z: 4, core: 2. Of those that a mesh axis runs over, the one named last changes fastest.
Arguments:
- cross_input: bfloat16 [4096, 3456], P(('grp', 'tbl')), may hold values from -6 to 6
- upstream: bfloat16 [4096, 3456], P(('grp', 'tbl')), may hold values from -6 to 6
- v_weight: bfloat16 [256, 3456], replicated, may hold values from -0.109375 to 0.109375
- u_weight: bfloat16 [256, 3456], replicated, may hold values from -0.375 to 0.375
- bias: float32 [3456], replicated, may hold values from -3 to 3
- placement: int32 [26], replicated, may hold values from 0 to 7, as said below
- owned_ids: int32 [40, 4, 4096], P('tbl', None, 'grp'), may hold values from 0 to 255
Outputs:
- cross_grad: float32 [256, 6912], P(('grp', 'tbl'))
- table_grad: float32 [40, 256, 128], P('tbl', 'grp')
Inputs may be any that keep to these rules, and one draw needn't show every extreme that they name: `placement`: no device holds more than 5 tables, and some device holds exactly 5.
All inputs are finite; a program needn't handle non-finite values.
Results may differ from a plain program's by a relative error of at most 0.004.
Values may be sent and summed in bfloat16 or wider, within the bound.
A program may use at most 64 MiB of HBM per device.

v0:
```python
import functools
import math

import jax
import jax.numpy as jnp
from jax import lax
from jax.experimental import pallas as pl
from jax.experimental.pallas import tpu as pltpu
from jax.sharding import PartitionSpec as P

EMB = 128
TABLES = 26
ROWS = 256
MESH = pl.DeviceIdType.MESH


def outer_sum(left, right):
    return jnp.einsum("br,bd->rd", left, right, preferred_element_type=jnp.float32)


def on_device(cross_input, upstream, v_weight, u_weight, bias, placement, owned_ids):
    n_grp = lax.axis_size("grp")
    n_tbl = lax.axis_size("tbl")
    samples = cross_input.shape[0]
    slots_dev = owned_ids.shape[0]
    scale = 1.0 / math.sqrt(samples * n_grp * n_tbl)
    hidden = jnp.dot(cross_input, v_weight.T, preferred_element_type=jnp.float32).astype(
        jnp.bfloat16
    )
    mixed = jnp.dot(hidden, u_weight, preferred_element_type=jnp.float32) + bias
    up_float = upstream.astype(jnp.float32)
    product_grad = (up_float * cross_input.astype(jnp.float32)).astype(jnp.bfloat16)
    hidden_grad = jnp.dot(product_grad, u_weight.T, preferred_element_type=jnp.float32).astype(
        jnp.bfloat16
    )
    input_grad = up_float * (1.0 + mixed) + jnp.dot(
        hidden_grad, v_weight, preferred_element_type=jnp.float32
    )
    pooled = input_grad[:, EMB:].astype(jnp.bfloat16).reshape(samples, TABLES, EMB)
    same = placement[:, None] == placement[None, :]
    earlier = jnp.arange(TABLES)[None, :] < jnp.arange(TABLES)[:, None]
    slot = jnp.sum((same & earlier).astype(jnp.int32), axis=1)
    target = slot * n_tbl + placement
    select = (jnp.arange(slots_dev * n_tbl, dtype=jnp.int32)[:, None] == target[None, :]).astype(
        jnp.bfloat16
    )
    outgoing = jnp.einsum("st,bte->sbe", select, pooled, preferred_element_type=jnp.float32)
    outgoing = outgoing.astype(jnp.bfloat16).reshape(slots_dev, n_tbl, samples, EMB)
    arriving = lax.all_to_all(outgoing, "tbl", split_axis=1, concat_axis=1, tiled=True)
    arriving = arriving.reshape(slots_dev, n_tbl * samples, EMB)
    row_numbers = jnp.arange(ROWS, dtype=jnp.int32)
    counts = jnp.sum(
        (owned_ids[:, :, None, :] == row_numbers[None, None, :, None]).astype(jnp.bfloat16), axis=1
    )
    row_terms = jnp.einsum("srm,sme->sre", counts, arriving, preferred_element_type=jnp.float32)
    table_grad = lax.psum_scatter(row_terms, "grp", scatter_dimension=1, tiled=True)
    term = jnp.concatenate(
        [outer_sum(hidden, product_grad), outer_sum(hidden_grad, cross_input)], axis=1
    )
    summed = lax.psum_scatter(term, ("grp", "tbl"), scatter_dimension=0, tiled=True)
    cross_grad = summed * scale
    return (cross_grad, table_grad)


def halving_fits(n_grp, n_tbl):
    return n_grp == 4 and n_tbl == 8


def scratch_of(samples, width, rank, n_tbl, slots_dev, hot, part, cuts):
    f32, bf16, i32 = jnp.float32, jnp.bfloat16, jnp.int32
    V, half = pltpu.VMEM, part // 2
    tab = (slots_dev, half, EMB)
    out = {
        "ci": V((2, samples, width), bf16),
        "up": V((2, samples, width), bf16),
        "v": V((rank, width), bf16),
        "u": V((rank, width), bf16),
        "pg": V((2, samples, width), bf16),
        "hid": V((2 * samples, rank), bf16),
        "hgr": V((2 * samples, rank), bf16),
        "hid_t": V((2, rank, samples), bf16),
        "hgr_t": V((2, rank, samples), bf16),
        "ids": V((2, n_tbl, slots_dev, hot, samples), i32),
        "slot": pltpu.SMEM((TABLES,), i32),
        "inv": pltpu.SMEM((slots_dev * n_tbl,), i32),
        "load_sem": pltpu.SemaphoreType.DMA((4,)),
        "in_s": pltpu.SemaphoreType.DMA((10,)),
        "in_r": pltpu.SemaphoreType.DMA((10,)),
        "id_s": pltpu.SemaphoreType.DMA((2, n_tbl)),
        "id_r": pltpu.SemaphoreType.DMA((2, n_tbl)),
        "ssem": pltpu.SemaphoreType.DMA((20,)),
        "rsem": pltpu.SemaphoreType.DMA((20,)),
    }
    lead = ((2, 2, 2), (2, 2), (2,), ())
    for name, tile in (
        ("a", (16, cuts[1] - cuts[0])),
        ("b", (16, cuts[2] - cuts[1])),
        ("e", (16, cuts[3] - cuts[2])),
        ("c", tab),
        ("d", tab),
    ):
        for k in range(4):
            shape = lead[k] + tile
            if name in "cd" and k == 0:
                shape = (TABLES, half, EMB)
            out["s%s%d" % (name, k)] = V(shape, bf16)
            out["r%s%d" % (name, k)] = V(shape, bf16)
            out["o%s%d" % (name, k)] = V(shape, f32)
    return out


def fused_body(n_grp, n_tbl, scale, cuts, names, *refs):
    f32, bf16 = jnp.float32, jnp.bfloat16
    ci_hbm, up_hbm, v_hbm, u_hbm, bias_ref, place_ref, ids_hbm, cross_ref, table_ref = refs[:9]
    r = dict(zip(names, refs[9:]))
    g = lax.axis_index("grp")
    t = lax.axis_index("tbl")
    core, x = g % 2, g // 2
    y, zl, zh = t % 2, (t // 2) % 2, t // 4
    og = g + 1 - 2 * core
    xg = core + 2 * (1 - x)
    yt = t + 1 - 2 * y
    zlt = t + 2 * (1 - 2 * zl)
    zht = t + 4 * (1 - 2 * zh)
    samples, width = ci_hbm.shape
    rank = v_hbm.shape[0]
    slots_dev = ids_hbm.shape[0]
    part = ROWS // n_grp
    half = part // 2

    barrier = pltpu.get_barrier_semaphore()

    def greet(gg, tt):
        pl.semaphore_signal(barrier, inc=1, device_id=(gg, tt), device_id_type=MESH)

    for step in range(1, n_tbl):
        greet(g, (t + step) % n_tbl)
        greet(og, (t + step) % n_tbl)
    greet(og, t)
    greet(xg, t)

    loads = [
        pltpu.make_async_copy(src, dst, r["load_sem"].at[i])
        for i, (src, dst) in enumerate(
            ((ci_hbm, r["ci"].at[0]), (v_hbm, r["v"]), (up_hbm, r["up"].at[0]), (u_hbm, r["u"]))
        )
    ]
    for load in loads:
        load.start()

    places = [place_ref[i] for i in range(TABLES)]
    targets = []
    for i in range(TABLES):
        slot = jnp.int32(0)
        for j in range(i):
            slot += (places[j] == places[i]).astype(jnp.int32)
        r["slot"][i] = jnp.minimum(slot, slots_dev - 1)
        targets.append(places[i] * slots_dev + slot)
    for q in range(slots_dev * n_tbl):
        which = jnp.int32(-1)
        for i in range(TABLES):
            which = jnp.where(targets[i] == q, i, which)
        r["inv"][q] = which

    nt = (((1,), (1,)), ((), ()))
    own_rows, their_rows = pl.ds(0, samples), pl.ds(samples, samples)
    loads[0].wait()
    loads[1].wait()
    hidden = lax.dot_general(r["ci"][0], r["v"][...], nt, preferred_element_type=f32)
    r["hid"][own_rows, :] = hidden.astype(bf16)
    r["hid_t"][0] = hidden.T.astype(bf16)
    loads[2].wait()
    loads[3].wait()
    r["pg"][0] = (r["up"][0].astype(f32) * r["ci"][0].astype(f32)).astype(bf16)
    hgrad = lax.dot_general(r["pg"][0], r["u"][...], nt, preferred_element_type=f32)
    r["hgr"][own_rows, :] = hgrad.astype(bf16)
    r["hgr_t"][0] = hgrad.T.astype(bf16)

    pl.semaphore_wait(barrier, 2 * n_tbl)

    def remote(src, dst, s, rs, gg, tt):
        copy = pltpu.make_async_remote_copy(
            src_ref=src, dst_ref=dst, send_sem=s, recv_sem=rs,
            device_id=(gg, tt), device_id_type=MESH,
        )
        copy.start()
        return copy

    pieces = [pl.ds(cuts[i], cuts[i + 1] - cuts[i]) for i in range(3)]
    moves = [(r["hid_t"].at[0], r["hid_t"].at[1]), (r["hgr_t"].at[0], r["hgr_t"].at[1])]
    for cols in pieces:
        moves.append((ci_hbm.at[:, cols], r["ci"].at[1, :, cols]))
        moves.append((up_hbm.at[:, cols], r["up"].at[1, :, cols]))
    moves.append((r["hid"].at[own_rows], r["hid"].at[their_rows]))
    moves.append((r["hgr"].at[own_rows], r["hgr"].at[their_rows]))
    in_copies = [
        remote(src, dst, r["in_s"].at[i], r["in_r"].at[i], og, t)
        for i, (src, dst) in enumerate(moves)
    ]
    id_copies = []
    for step in range(n_tbl):
        to = (t + step) % n_tbl
        block = ids_hbm.at[:, :, pl.ds(pl.multiple_of(to * samples, samples), samples)]
        if step == 0:
            mine = pltpu.make_async_copy(block, r["ids"].at[0, t], r["id_s"].at[0, 0])
            mine.start()
        else:
            id_copies.append(
                remote(block, r["ids"].at[0, t], r["id_s"].at[0, step], r["id_r"].at[0, step], g, to)
            )
        id_copies.append(
            remote(block, r["ids"].at[1, t], r["id_s"].at[1, step], r["id_r"].at[1, step], og, to)
        )

    quarter = rank // n_grp

    def picked(ref):
        both = []
        for who in range(2):
            for start in (core + 2 * x, core + 2 - 2 * x):
                at = pl.ds(pl.multiple_of(start * quarter, quarter), quarter)
                both.append(ref[who, at, :])
        return [jnp.concatenate(both[:2], axis=0), jnp.concatenate(both[2:], axis=0)]

    in_copies[0].wait()
    in_copies[1].wait()
    hsel, gsel = picked(r["hid_t"]), picked(r["hgr_t"])

    def blocks(lo, hi):
        theirs = r["ci"][1, :, lo:hi]
        product = (r["up"][1, :, lo:hi].astype(f32) * theirs.astype(f32)).astype(bf16)
        left = jnp.dot(hsel[0], r["pg"][0, :, lo:hi], preferred_element_type=f32)
        left += jnp.dot(hsel[1], product, preferred_element_type=f32)
        right = jnp.dot(gsel[0], r["ci"][0, :, lo:hi], preferred_element_type=f32)
        right += jnp.dot(gsel[1], theirs, preferred_element_type=f32)
        return [
            jnp.concatenate([left[8 * d : 8 * d + 8], right[8 * d : 8 * d + 8]], axis=0)
            for d in range(2 * n_tbl)
        ]

    in_copies[2].wait()
    in_copies[3].wait()
    for lo in range(cuts[0], cuts[1], 512):
        hi = min(lo + 512, cuts[1])
        made = blocks(lo, hi)
        for d in range(n_tbl):
            at = (d // 4, (d // 2) % 2, d % 2, slice(None), slice(lo, hi))
            r["oa0"][at] = made[d]
            r["sa0"][at] = made[n_tbl + d].astype(bf16)
    sems = iter(range(20))

    def send(name, k, gg, tt):
        i = next(sems)
        return remote(
            r["s%s%d" % (name, k)], r["r%s%d" % (name, k)], r["ssem"].at[i], r["rsem"].at[i], gg, tt
        )

    a0 = send("a", 0, xg, t)
    in_copies[4].wait()
    in_copies[5].wait()
    for lo in range(cuts[1], cuts[2], 512):
        hi = min(lo + 512, cuts[2])
        made = blocks(lo, hi)
        for side in range(2):
            xx = x if side == 0 else 1 - x
            for z in range(n_tbl // 2):
                even, odd = made[side * n_tbl + 2 * z], made[side * n_tbl + 2 * z + 1]
                at = (xx, z // 2, z % 2, slice(None), slice(lo - cuts[1], hi - cuts[1]))
                r["ob0"][at] = jnp.where(y == 0, even, odd)
                r["sb0"][at] = jnp.where(y == 0, odd, even).astype(bf16)
    b0 = send("b", 0, g, yt)
    in_copies[6].wait()
    in_copies[7].wait()
    for lo in range(cuts[2], cuts[3], 512):
        hi = min(lo + 512, cuts[3])
        made = blocks(lo, hi)
        for side in range(2):
            xx = x if side == 0 else 1 - x
            for z in range(2):
                for yy in range(2):
                    first = side * n_tbl + 4 * z + yy
                    at = (xx, z, yy, slice(None), slice(lo - cuts[2], hi - cuts[2]))
                    r["oe0"][at] = jnp.where(zl == 0, made[first], made[first + 2])
                    r["se0"][at] = jnp.where(zl == 0, made[first + 2], made[first]).astype(bf16)
    e0 = send("e", 0, g, zlt)

    def indices(depth):
        out = [()]
        for _ in range(depth):
            out = [i + (j,) for i in out for j in range(2)]
        return out

    def halve(name, k, axis, bit, gg, tt, before):
        before.wait()
        own, came = r["o%s%d" % (name, k)], r["r%s%d" % (name, k)]
        kept, out = r["o%s%d" % (name, k + 1)], r["s%s%d" % (name, k + 1)]

        def where_to(i, b):
            return i[:axis] + (b,) + i[axis:]

        def fill(dst, b, kind):
            for i in indices(2 - k):
                at = where_to(i, b)
                value = own[at] + came[at].astype(f32)
                if i:
                    dst[i] = value.astype(kind)
                else:
                    dst[...] = value.astype(kind)

        fill(out, 1 - bit, bf16)
        copy = send(name, k + 1, gg, tt)
        fill(kept, bit, f32)
        return copy

    index = lax.broadcasted_iota(jnp.int32, (2 * part, samples), 0)
    side_of = jnp.where(index // part == 0, x, 1 - x)
    row_of = (side_of * 2 + core) * part + index % part

    def tables(pair, carry):
        cols = pl.ds(pl.multiple_of(EMB + pair * 2 * EMB, EMB), 2 * EMB)
        shift = jnp.concatenate(
            [bias_ref[pl.ds(1 + 2 * pair, 1), :], bias_ref[pl.ds(2 + 2 * pair, 1), :]], axis=1
        )
        mixed = jnp.dot(r["hid"][...], r["u"][:, cols], preferred_element_type=f32) + shift
        back = jnp.dot(r["hgr"][...], r["v"][:, cols], preferred_element_type=f32)
        up_all = jnp.concatenate([r["up"][0, :, cols], r["up"][1, :, cols]], axis=0).astype(f32)
        pooled = (up_all * (1.0 + mixed) + back).astype(bf16)
        for piece in range(2):
            table = pair * 2 + piece
            owner, slot = place_ref[table], r["slot"][table]
            sums = jnp.zeros((2 * part, EMB), f32)
            for who in range(2):
                looked = r["ids"][who, owner, slot]
                count = jnp.zeros((2 * part, samples), f32)
                for k in range(looked.shape[0]):
                    count += jnp.where(looked[k : k + 1, :] == row_of, 1.0, 0.0)
                sums += jnp.dot(
                    count.astype(bf16),
                    pooled[who * samples : (who + 1) * samples, piece * EMB : (piece + 1) * EMB],
                    preferred_element_type=f32,
                )
            r["oc0"][table] = sums[:half]
            r["sc0"][table] = sums[part : part + half].astype(bf16)
            r["od0"][table] = sums[half:part]
            r["sd0"][table] = sums[part + half :].astype(bf16)
        return carry

    in_copies[8].wait()
    in_copies[9].wait()
    mine.wait()
    for copy in id_copies:
        copy.wait()
    lax.fori_loop(0, TABLES // 2, tables, 0)
    c0 = send("c", 0, xg, t)
    d0 = send("d", 0, xg, t)

    def each_slot(yy, put):
        def run(i, carry):
            owner = i // slots_dev * 2 + yy
            which = r["inv"][owner * slots_dev + i % slots_dev]
            there = jnp.where(which >= 0, 1.0, 0.0)
            z = i // slots_dev
            put((z // 2, z % 2, i % slots_dev), jnp.maximum(which, 0), there)
            return carry

        lax.fori_loop(0, slots_dev * n_tbl // 2, run, 0)

    def put(name, dst, kind):
        def store(at, which, there):
            value = r["o%s0" % name][which] + r["r%s0" % name][which].astype(f32)
            dst[at] = (value * there).astype(kind)

        return store

    def spread(name, before):
        before.wait()
        each_slot(1 - y, put(name, r["s%s1" % name], bf16))
        copy = send(name, 1, g, yt)
        each_slot(y, put(name, r["o%s1" % name], f32))
        return copy

    a1 = halve("a", 0, 2, y, g, yt, a0)
    e1 = halve("e", 0, 1, zh, g, zht, e0)
    b1 = halve("b", 0, 0, x, xg, t, b0)
    c1 = spread("c", c0)
    a2 = halve("a", 1, 1, zl, g, zlt, a1)
    e2 = halve("e", 1, 0, x, xg, t, e1)
    d1 = spread("d", d0)
    a3 = halve("a", 2, 0, zh, g, zht, a2)
    c2 = halve("c", 1, 1, zl, g, zlt, c1)
    b2 = halve("b", 1, 1, zl, g, zlt, b1)
    e3 = halve("e", 2, 0, y, g, yt, e2)
    d2 = halve("d", 1, 1, zl, g, zlt, d1)
    c3 = halve("c", 2, 0, zh, g, zht, c2)
    b3 = halve("b", 2, 0, zh, g, zht, b2)
    d3 = halve("d", 2, 0, zh, g, zht, d2)

    def total(name):
        return r["o%s3" % name][...] + r["r%s3" % name][...].astype(f32)

    def finish(value, lo, hi):
        value = value * scale
        cross_ref[:, lo:hi] = value[:8]
        cross_ref[:, width + lo : width + hi] = value[8:]

    for name, copy, i in (("a", a3, 0), ("b", b3, 1), ("e", e3, 2)):
        copy.wait()
        finish(total(name), cuts[i], cuts[i + 1])
    c3.wait()
    table_ref[:, :half, :] = total("c")
    d3.wait()
    table_ref[:, half:, :] = total("d")


def copy_body(cross_ref, table_ref, cross_out, table_out):
    cross_out[...] = cross_ref[...]
    table_out[...] = table_ref[...]


def on_device_fused(cross_input, upstream, v_weight, u_weight, bias, placement, owned_ids):
    n_grp = lax.axis_size("grp")
    n_tbl = lax.axis_size("tbl")
    samples, width = cross_input.shape
    rank = v_weight.shape[0]
    slots_dev, hot = owned_ids.shape[:2]
    scale = 1.0 / math.sqrt(samples * n_grp * n_tbl)
    part = ROWS // n_grp
    tiles = width // EMB
    cuts = (0, tiles * 7 // 27 * EMB, tiles * 18 // 27 * EMB, width)
    scratch = scratch_of(samples, width, rank, n_tbl, slots_dev, hot, part, cuts)
    vmem = pl.BlockSpec(memory_space=pltpu.VMEM)
    smem = pl.BlockSpec(memory_space=pltpu.SMEM)
    hbm = pl.BlockSpec(memory_space=pl.ANY)
    shapes = (
        jax.ShapeDtypeStruct((rank // (n_grp * n_tbl), 2 * width), jnp.float32),
        jax.ShapeDtypeStruct((slots_dev, part, EMB), jnp.float32),
    )
    sums = pl.pallas_call(
        functools.partial(fused_body, n_grp, n_tbl, scale, cuts, tuple(scratch)),
        out_shape=shapes,
        in_specs=[hbm] * 4 + [vmem, smem, hbm],
        out_specs=(vmem, vmem),
        scratch_shapes=list(scratch.values()),
        compiler_params=pltpu.CompilerParams(
            collective_id=0, has_side_effects=True, vmem_limit_bytes=60 * 1024 * 1024
        ),
        name="cross_backward",
    )(
        cross_input, upstream, v_weight, u_weight,
        bias.reshape(width // EMB, EMB), placement, owned_ids,
    )
    return pl.pallas_call(
        copy_body,
        out_shape=shapes,
        in_specs=[vmem, vmem],
        out_specs=(vmem, vmem),
        name="hand_over",
    )(*sums)


def solution(mesh):
    in_specs = (
        P(("grp", "tbl"), None),
        P(("grp", "tbl"), None),
        P(),
        P(),
        P(),
        P(),
        P("tbl", None, "grp"),
    )
    out_specs = (P(("grp", "tbl"), None), P("tbl", "grp", None))
    fused = halving_fits(mesh.shape["grp"], mesh.shape["tbl"])
    return jax.shard_map(
        on_device_fused if fused else on_device, mesh=mesh, in_specs=in_specs, out_specs=out_specs, check_vma=False
    )
```

profile of v0, /device:TPU:0, one launch (start us, length us, event | category | flops | bytes accessed | tf_op | source)
XLA Modules:
  0.0 50.3 jit_solution(14411809881777867022)
XLA Ops:
  0.6 47.9 %cross_backward.1 = (f32[8,6912]{1,0:T(8,128)}, f32[5,64,128]{2,1,0:T(8,128)}) custom-call(bf16[128,3456]{1,0:T(8,128)(2,1)} %refs_0_.1, bf16[128,3456]{1,0:T(8,128)(2,1)} %refs_1_.1, bf16[256,3456]{1,0:T(8,128)(2,1)} %refs_2_.1, bf16[256,3456]{1,0:T(8,128)(2,1)} %refs_3_.1, f32[27,128]{1,0:T(8,128)} %bitcast.1, s32[26]{0:T(128)} %refs_5_.1, ...), custom_call_target="tpu_custom_call" | custom-call | tf_op jit(solution)/shard_map/cross_backward/pallas_call | solution.py:438
  48.6 1.8 %hand_over.1 = (f32[8,6912]{1,0:T(8,128)}, f32[5,64,128]{2,1,0:T(8,128)}) custom-call(f32[8,6912]{1,0:T(8,128)} %get-tuple-element.4.cross_ref, f32[5,64,128]{2,1,0:T(8,128)} %get-tuple-element.5.table_ref), custom_call_target="tpu_custom_call" | custom-call | tf_op jit(solution)/shard_map/hand_over/pallas_call | solution.py:452
where the time goes:
time: 50.6 us; the launch traced here: 50.3 us
  Pallas kernels  49.7 us (98%)
  between operations  0.64 us (1%)
    pallas_call x1, Pallas kernels, on_device_fused(): pl.pallas_call(functools.partial(fused_body, n_grp, n_tbl, scale, cuts, t...  47.9 us
    pallas_call x1, Pallas kernels, on_device_fused(): pl.pallas_call(copy_body, out_shape=shapes, in_specs=[vmem, vmem], out_sp...  1.78 us

commit v1 on v0

v1 whole, which is shorter than its diff:
```python
import functools
import math

import jax
import jax.numpy as jnp
from jax import lax
from jax.experimental import pallas as pl
from jax.experimental.pallas import tpu as pltpu
from jax.sharding import PartitionSpec as P

EMB = 128
TABLES = 26
ROWS = 256
MESH = pl.DeviceIdType.MESH


def outer_sum(left, right):
    return jnp.einsum("br,bd->rd", left, right, preferred_element_type=jnp.float32)


def on_device(cross_input, upstream, v_weight, u_weight, bias, placement, owned_ids):
    n_grp = lax.axis_size("grp")
    n_tbl = lax.axis_size("tbl")
    samples = cross_input.shape[0]
    slots_dev = owned_ids.shape[0]
    scale = 1.0 / math.sqrt(samples * n_grp * n_tbl)
    hidden = jnp.dot(cross_input, v_weight.T, preferred_element_type=jnp.float32).astype(
        jnp.bfloat16
    )
    mixed = jnp.dot(hidden, u_weight, preferred_element_type=jnp.float32) + bias
    up_float = upstream.astype(jnp.float32)
    product_grad = (up_float * cross_input.astype(jnp.float32)).astype(jnp.bfloat16)
    hidden_grad = jnp.dot(product_grad, u_weight.T, preferred_element_type=jnp.float32).astype(
        jnp.bfloat16
    )
    input_grad = up_float * (1.0 + mixed) + jnp.dot(
        hidden_grad, v_weight, preferred_element_type=jnp.float32
    )
    pooled = input_grad[:, EMB:].astype(jnp.bfloat16).reshape(samples, TABLES, EMB)
    same = placement[:, None] == placement[None, :]
    earlier = jnp.arange(TABLES)[None, :] < jnp.arange(TABLES)[:, None]
    slot = jnp.sum((same & earlier).astype(jnp.int32), axis=1)
    target = slot * n_tbl + placement
    select = (jnp.arange(slots_dev * n_tbl, dtype=jnp.int32)[:, None] == target[None, :]).astype(
        jnp.bfloat16
    )
    outgoing = jnp.einsum("st,bte->sbe", select, pooled, preferred_element_type=jnp.float32)
    outgoing = outgoing.astype(jnp.bfloat16).reshape(slots_dev, n_tbl, samples, EMB)
    arriving = lax.all_to_all(outgoing, "tbl", split_axis=1, concat_axis=1, tiled=True)
    arriving = arriving.reshape(slots_dev, n_tbl * samples, EMB)
    row_numbers = jnp.arange(ROWS, dtype=jnp.int32)
    counts = jnp.sum(
        (owned_ids[:, :, None, :] == row_numbers[None, None, :, None]).astype(jnp.bfloat16), axis=1
    )
    row_terms = jnp.einsum("srm,sme->sre", counts, arriving, preferred_element_type=jnp.float32)
    table_grad = lax.psum_scatter(row_terms, "grp", scatter_dimension=1, tiled=True)
    term = jnp.concatenate(
        [outer_sum(hidden, product_grad), outer_sum(hidden_grad, cross_input)], axis=1
    )
    summed = lax.psum_scatter(term, ("grp", "tbl"), scatter_dimension=0, tiled=True)
    cross_grad = summed * scale
    return (cross_grad, table_grad)


def halving_fits(n_grp, n_tbl):
    return n_grp == 4 and n_tbl == 8


CANON = "xhly"


def left_over(done):
    return [d for d in CANON if d not in done]


def lead_of(done):
    return (2,) * len(left_over(done))


def plan_of(width):
    tiles = width // EMB
    ends = [tiles * n // 27 * EMB for n in (0, 6, 9, 13, 16, 20, 24, 27)]
    dims = ("yxlh", "lhyx", "yxlh", "lhyx", "lhxy", "ylxh", "ylxh")
    cross = {}
    for i, name in enumerate("abcdefg"):
        cross[name] = (("u", ends[i]), ("v", ends[i]), ends[i + 1] - ends[i], dims[i])
    table = {}
    for i, rest in enumerate(("yhl", "ylh", "ylh", "lyh")):
        table["ABCD"[i]] = (i, i + 1, "x" + rest)
    groups = (0, 8, 16, 22, 26)
    order = (
        ["Xb", "Xg", "T0", "Xa", "Xd", "T1", "Xf", "Xe", "Xc", "T2", "T3", "b1", "g1", "d1", "a1", "e1", "b2", "g2", "f1", "A1", "B1", "C1", "D1", "d2", "c1", "a2", "b3", "g3", "f2", "e2", "A2", "c2", "D2", "b4", "B2", "e3", "a3", "f3", "g4", "C2", "d3", "c3", "A3", "D3", "B3", "e4", "d4", "a4", "f4", "C3", "A4", "c4", "B4", "D4", "C4"]
    )
    return cross, table, groups, order


def scratch_of(samples, width, rank, n_tbl, slots_dev, hot, part, plan):
    f32, bf16, i32 = jnp.float32, jnp.bfloat16, jnp.int32
    V = pltpu.VMEM
    cross, table, groups, order = plan
    rows = part // len(table)
    out = {
        "ci": V((2 * samples, width), bf16),
        "up": V((2 * samples, width), bf16),
        "v": V((rank, width), bf16),
        "u": V((rank, width), bf16),
        "pg": V((2 * samples, width), bf16),
        "hid": V((2 * samples, rank), bf16),
        "hgr": V((2 * samples, rank), bf16),
        "hid_t": V((2, rank, samples), bf16),
        "hgr_t": V((2, rank, samples), bf16),
        "ids": V((2, n_tbl, slots_dev, hot, samples), i32),
        "slot": pltpu.SMEM((TABLES,), i32),
        "inv": pltpu.SMEM((slots_dev * n_tbl,), i32),
        "load_sem": pltpu.SemaphoreType.DMA((4,)),
        "in_s": pltpu.SemaphoreType.DMA((10,)),
        "in_r": pltpu.SemaphoreType.DMA((10,)),
        "id_s": pltpu.SemaphoreType.DMA((2, n_tbl)),
        "id_r": pltpu.SemaphoreType.DMA((2, n_tbl)),
        "ssem": pltpu.SemaphoreType.DMA((64,)),
        "rsem": pltpu.SemaphoreType.DMA((64,)),
        "st": V((TABLES, part, EMB), bf16),
        "rt": V((TABLES, part, EMB), bf16),
        "ot": V((TABLES, part, EMB), f32),
    }
    for name, (top, bottom, wide, dims) in cross.items():
        for k in range(4):
            shape = lead_of(dims[: k + 1]) + (16, wide)
            out["s%s%d" % (name, k)] = V(shape, bf16)
            out["r%s%d" % (name, k)] = V(shape, bf16)
            out["o%s%d" % (name, k)] = V(shape, f32)
    for name, (lo, hi, dims) in table.items():
        for k in range(1, 4):
            shape = lead_of(dims[: k + 1]) + (slots_dev, rows, EMB)
            out["s%s%d" % (name, k)] = V(shape, bf16)
            out["r%s%d" % (name, k)] = V(shape, bf16)
            out["o%s%d" % (name, k)] = V(shape, f32)
    return out


def fused_body(n_grp, n_tbl, scale, plan, names, *refs):
    f32, bf16 = jnp.float32, jnp.bfloat16
    ci_hbm, up_hbm, v_hbm, u_hbm, bias_ref, place_ref, ids_hbm, cross_ref, table_ref = refs[:9]
    r = dict(zip(names, refs[9:]))
    cross, table, groups, order = plan
    g = lax.axis_index("grp")
    t = lax.axis_index("tbl")
    core, x = g % 2, g // 2
    y, zl, zh = t % 2, (t // 2) % 2, t // 4
    og = g + 1 - 2 * core
    bits = {"x": x, "h": zh, "l": zl, "y": y}
    peers = {
        "x": (core + 2 * (1 - x), t),
        "y": (g, t + 1 - 2 * y),
        "l": (g, t + 2 * (1 - 2 * zl)),
        "h": (g, t + 4 * (1 - 2 * zh)),
    }
    samples, width = ci_hbm.shape
    rank = v_hbm.shape[0]
    slots_dev = ids_hbm.shape[0]
    part = ROWS // n_grp
    rows = part // len(table)
    quarter = rank // n_grp

    barrier = pltpu.get_barrier_semaphore()

    def greet(gg, tt):
        pl.semaphore_signal(barrier, inc=1, device_id=(gg, tt), device_id_type=MESH)

    for step in range(1, n_tbl):
        greet(g, (t + step) % n_tbl)
        greet(og, (t + step) % n_tbl)
    greet(og, t)
    greet(*peers["x"])

    own_rows, their_rows = pl.ds(0, samples), pl.ds(samples, samples)
    loads = [
        pltpu.make_async_copy(src, dst, r["load_sem"].at[i])
        for i, (src, dst) in enumerate(
            (
                (ci_hbm, r["ci"].at[own_rows]),
                (v_hbm, r["v"]),
                (up_hbm, r["up"].at[own_rows]),
                (u_hbm, r["u"]),
            )
        )
    ]
    for load in loads:
        load.start()

    pl.semaphore_wait(barrier, 2 * n_tbl)

    def remote(src, dst, s, rs, peer):
        copy = pltpu.make_async_remote_copy(
            src_ref=src, dst_ref=dst, send_sem=s, recv_sem=rs,
            device_id=peer, device_id_type=MESH,
        )
        copy.start()
        return copy

    sems = iter(range(64))

    def send(src, dst, peer):
        i = next(sems)
        return remote(src, dst, r["ssem"].at[i], r["rsem"].at[i], peer)

    thirds = [width // EMB * i // 3 * EMB for i in range(4)]
    moves = []
    for i in range(3):
        cols = pl.ds(thirds[i], thirds[i + 1] - thirds[i])
        moves.append((ci_hbm.at[:, cols], r["ci"].at[their_rows, cols]))
        moves.append((up_hbm.at[:, cols], r["up"].at[their_rows, cols]))
    raw = [
        remote(src, dst, r["in_s"].at[i], r["in_r"].at[i], (og, t))
        for i, (src, dst) in enumerate(moves)
    ]
    id_copies = []
    for step in range(n_tbl):
        to = (t + step) % n_tbl
        block = ids_hbm.at[:, :, pl.ds(pl.multiple_of(to * samples, samples), samples)]
        if step == 0:
            mine = pltpu.make_async_copy(block, r["ids"].at[0, t], r["id_s"].at[0, 0])
            mine.start()
        else:
            id_copies.append(
                remote(
                    block, r["ids"].at[0, t], r["id_s"].at[0, step], r["id_r"].at[0, step], (g, to)
                )
            )
        id_copies.append(
            remote(block, r["ids"].at[1, t], r["id_s"].at[1, step], r["id_r"].at[1, step], (og, to))
        )

    nt = (((1,), (1,)), ((), ()))

    def by_position(value):
        blocks = []
        for gg in range(n_grp):
            for pos in range(n_tbl):
                yy, ll, hh = pos // 4, (pos // 2) % 2, pos % 2
                at = gg * quarter + 8 * (hh * 4 + ll * 2 + yy)
                blocks.append(value[at : at + 8])
        return jnp.concatenate(blocks, axis=0).astype(bf16)

    loads[0].wait()
    loads[1].wait()
    hidden = lax.dot_general(r["ci"][own_rows, :], r["v"][...], nt, preferred_element_type=f32)
    r["hid"][own_rows, :] = hidden.astype(bf16)
    r["hid_t"][0] = by_position(hidden.T)
    at = 6
    ready = []
    for i, (src, dst) in enumerate(
        (
            (r["hid_t"].at[0], r["hid_t"].at[1]),
            (r["hid"].at[own_rows], r["hid"].at[their_rows]),
        )
    ):
        ready.append(remote(src, dst, r["in_s"].at[at + i], r["in_r"].at[at + i], (og, t)))
    loads[2].wait()
    loads[3].wait()
    places = [place_ref[i] for i in range(TABLES)]
    targets = []
    for i in range(TABLES):
        slot = jnp.int32(0)
        for j in range(i):
            slot += (places[j] == places[i]).astype(jnp.int32)
        r["slot"][i] = jnp.minimum(slot, slots_dev - 1)
        targets.append(places[i] * slots_dev + slot)
    for q in range(slots_dev * n_tbl):
        which = jnp.int32(-1)
        for i in range(TABLES):
            which = jnp.where(targets[i] == q, i, which)
        r["inv"][q] = which
    r["pg"][own_rows, :] = (
        r["up"][own_rows, :].astype(f32) * r["ci"][own_rows, :].astype(f32)
    ).astype(bf16)
    hgrad = lax.dot_general(r["pg"][own_rows, :], r["u"][...], nt, preferred_element_type=f32)
    r["hgr"][own_rows, :] = hgrad.astype(bf16)
    r["hgr_t"][0] = by_position(hgrad.T)
    for i, (src, dst) in enumerate(
        (
            (r["hgr_t"].at[0], r["hgr_t"].at[1]),
            (r["hgr"].at[own_rows], r["hgr"].at[their_rows]),
        )
    ):
        ready.append(remote(src, dst, r["in_s"].at[at + 2 + i], r["in_r"].at[at + 2 + i], (og, t)))

    index = lax.broadcasted_iota(jnp.int32, (2 * part, 2 * samples), 0)
    side_of = jnp.where(index // part == 0, x, 1 - x)
    row_of = ((side_of * 2 + core) * part + index % part).astype(f32).astype(bf16)

    def tables(pair):
        cols = pl.ds(EMB + pair * 2 * EMB, 2 * EMB)
        shift = jnp.concatenate(
            [bias_ref[pl.ds(1 + 2 * pair, 1), :], bias_ref[pl.ds(2 + 2 * pair, 1), :]], axis=1
        )
        mixed = jnp.dot(r["hid"][...], r["u"][:, cols], preferred_element_type=f32) + shift
        back = jnp.dot(r["hgr"][...], r["v"][:, cols], preferred_element_type=f32)
        pooled = (r["up"][:, cols].astype(f32) * (1.0 + mixed) + back).astype(bf16)
        for piece in range(2):
            which = pair * 2 + piece
            owner, slot = place_ref[which], r["slot"][which]
            looked = jnp.concatenate([r["ids"][0, owner, slot], r["ids"][1, owner, slot]], axis=1)
            looked = looked.astype(f32).astype(bf16)
            one, zero = jnp.bfloat16(1), jnp.bfloat16(0)
            count = jnp.zeros((2 * part, 2 * samples), bf16)
            for k in range(looked.shape[0]):
                count += jnp.where(looked[k : k + 1, :] == row_of, one, zero)
            sums = jnp.dot(
                count, pooled[:, piece * EMB : (piece + 1) * EMB], preferred_element_type=f32
            )
            r["ot"][which] = sums[:part]
            r["st"][which] = sums[part:].astype(bf16)

    def picked(ref, first):
        def take(gg, start, size):
            at = pl.ds(pl.multiple_of(gg * quarter + start, size), size)
            return jnp.concatenate([ref[0, at, :], ref[1, at, :]], axis=1)

        out = []
        for side in range(2):
            bit = bits[first] if side == 0 else 1 - bits[first]
            if first == "x":
                out.append(take(core + 2 * bit, 0, quarter))
                continue
            for xx in range(2):
                if first == "y":
                    out.append(take(core + 2 * xx, bit * (quarter // 2), quarter // 2))
                else:
                    for yy in range(2):
                        out.append(
                            take(
                                core + 2 * xx, yy * (quarter // 2) + bit * (quarter // 4), quarter // 4
                            )
                        )
        return jnp.concatenate(out, axis=0)

    def place_of(first, i):
        a, b, c = i // 4, (i // 2) % 2, i % 2
        if first == "y":
            return (a, c, b)
        if first == "l":
            return (a, c, b)
        return (c, b, a)

    flying, chosen, waited = {}, {}, set()

    def await_all(key, copies):
        if key not in waited:
            waited.add(key)
            for copy in copies:
                copy.wait()

    def raw_ready(lo, hi):
        for i in range(3):
            if lo < thirds[i + 1] and hi > thirds[i]:
                await_all("raw%d" % i, raw[2 * i : 2 * i + 2])

    made_pg = set()

    def factors(kind, first):
        index = 0 if kind == "u" else 2
        await_all("ready%d" % index, [ready[index]])
        if (kind, first) not in chosen:
            chosen[kind, first] = picked(r["hid_t" if kind == "u" else "hgr_t"], first)
        return chosen[kind, first]

    def product(kind, lhs, lo, hi):
        if kind == "v":
            return jnp.dot(lhs, r["ci"][:, lo:hi], preferred_element_type=f32)
        theirs = (
            r["up"][their_rows, lo:hi].astype(f32) * r["ci"][their_rows, lo:hi].astype(f32)
        ).astype(bf16)
        both = jnp.concatenate([r["pg"][own_rows, lo:hi], theirs], axis=0)
        return jnp.dot(lhs, both, preferred_element_type=f32)

    def cross_piece(name):
        top, bottom, wide, dims = cross[name]
        for kind, lo in (top, bottom):
            raw_ready(lo, lo + wide)
        for off in range(0, wide, 512):
            end = min(off + 512, wide)
            halves = []
            for kind, lo in (top, bottom):
                halves.append(product(kind, factors(kind, dims[0]), lo + off, lo + end))
            for i in range(2 * n_tbl):
                tile = jnp.concatenate([h[8 * i : 8 * i + 8] for h in halves], axis=0)
                at = place_of(dims[0], i % n_tbl) + (slice(None), slice(off, end))
                if i < n_tbl:
                    r["o%s0" % name][at] = tile
                else:
                    r["s%s0" % name][at] = tile.astype(bf16)
        flying[name] = send(r["s%s0" % name], r["r%s0" % name], peers[dims[0]])

    def table_group(n):
        await_all("ready1", [ready[1]])
        await_all("ready3", [ready[3]])
        raw_ready(EMB * (1 + groups[n]), EMB * (1 + groups[n + 1]))
        await_all("ids", [mine] + id_copies)
        for pair in range(groups[n] // 2, groups[n + 1] // 2):
            tables(pair)
        at = pl.ds(groups[n], groups[n + 1] - groups[n])
        flying["T%d" % n] = send(r["st"].at[at], r["rt"].at[at], peers["x"])

    def indices(depth):
        out = [()]
        for _ in range(depth):
            out = [i + (j,) for i in out for j in range(2)]
        return out

    def halve(name, dims, k):
        flying[name].wait()
        own, came = r["o%s%d" % (name, k)], r["r%s%d" % (name, k)]
        kept, out = r["o%s%d" % (name, k + 1)], r["s%s%d" % (name, k + 1)]
        axis = left_over(dims[: k + 1]).index(dims[k + 1])
        bit = bits[dims[k + 1]]

        def fill(dst, b, kind):
            for i in indices(2 - k):
                at = i[:axis] + (b,) + i[axis:]
                value = (own[at] + came[at].astype(f32)).astype(kind)
                if i:
                    dst[i] = value
                else:
                    dst[...] = value

        fill(out, 1 - bit, bf16)
        flying[name] = send(out, r["r%s%d" % (name, k + 1)], peers[dims[k + 1]])
        fill(kept, bit, f32)

    def spread(name):
        lo, hi, dims = table[name]
        for n in range(len(groups) - 1):
            await_all("T%d" % n, [flying["T%d" % n]])
        others = left_over(dims[:2])
        weight = {"h": 4, "l": 2, "y": 1}
        at_rows = pl.ds(lo * rows, (hi - lo) * rows)

        def each_slot(bit, dst, kind):
            def run(i, carry):
                z = i // slots_dev
                pair = (z // 2, z % 2)
                owner = bit * weight[dims[1]]
                for d, b in zip(others, pair):
                    owner += b * weight[d]
                which = r["inv"][owner * slots_dev + i % slots_dev]
                there = jnp.where(which >= 0, 1.0, 0.0)
                which = jnp.maximum(which, 0)
                value = r["ot"][which, at_rows, :] + r["rt"][which, at_rows, :].astype(f32)
                dst[pair + (i % slots_dev,)] = (value * there).astype(kind)
                return carry

            lax.fori_loop(0, slots_dev * n_tbl // 2, run, 0, unroll=5)

        bit = bits[dims[1]]
        each_slot(1 - bit, r["s%s1" % name], bf16)
        flying[name] = send(r["s%s1" % name], r["r%s1" % name], peers[dims[1]])
        each_slot(bit, r["o%s1" % name], f32)

    def finish(name):
        flying[name].wait()
        value = r["o%s3" % name][...] + r["r%s3" % name][...].astype(f32)
        if name in table:
            lo, hi, dims = table[name]
            table_ref[:, lo * rows : hi * rows, :] = value
        else:
            top, bottom, wide, dims = cross[name]
            value = value * scale
            for i, (kind, lo) in enumerate((top, bottom)):
                at = lo if kind == "u" else width + lo
                cross_ref[:, at : at + wide] = value[8 * i : 8 * i + 8]

    for step in order:
        kind, rest = step[0], step[1:]
        if kind == "T":
            table_group(int(rest))
        elif kind == "X":
            cross_piece(rest)
        elif rest == "4":
            finish(kind)
        elif rest == "1" and kind in table:
            spread(kind)
        else:
            halve(kind, (table if kind in table else cross)[kind][-1], int(rest) - 1)


def copy_body(cross_ref, table_ref, cross_out, table_out, sems):
    copies = [
        pltpu.make_async_copy(cross_ref, cross_out, sems.at[0]),
        pltpu.make_async_copy(table_ref, table_out, sems.at[1]),
    ]
    for copy in copies:
        copy.start()
    for copy in copies:
        copy.wait()


def on_device_fused(cross_input, upstream, v_weight, u_weight, bias, placement, owned_ids):
    n_grp = lax.axis_size("grp")
    n_tbl = lax.axis_size("tbl")
    samples, width = cross_input.shape
    rank = v_weight.shape[0]
    slots_dev, hot = owned_ids.shape[:2]
    scale = 1.0 / math.sqrt(samples * n_grp * n_tbl)
    part = ROWS // n_grp
    plan = plan_of(width)
    scratch = scratch_of(samples, width, rank, n_tbl, slots_dev, hot, part, plan)
    vmem = pl.BlockSpec(memory_space=pltpu.VMEM)
    smem = pl.BlockSpec(memory_space=pltpu.SMEM)
    hbm = pl.BlockSpec(memory_space=pl.ANY)
    shapes = (
        jax.ShapeDtypeStruct((rank // (n_grp * n_tbl), 2 * width), jnp.float32),
        jax.ShapeDtypeStruct((slots_dev, part, EMB), jnp.float32),
    )
    sums = pl.pallas_call(
        functools.partial(fused_body, n_grp, n_tbl, scale, plan, tuple(scratch)),
        out_shape=tuple(pltpu.VMEM(s.shape, s.dtype) for s in shapes),
        in_specs=[hbm] * 4 + [vmem, smem, hbm],
        out_specs=(vmem, vmem),
        scratch_shapes=list(scratch.values()),
        compiler_params=pltpu.CompilerParams(
            collective_id=0, has_side_effects=True, vmem_limit_bytes=60 * 1024 * 1024
        ),
        name="cross_backward",
    )(
        cross_input, upstream, v_weight, u_weight,
        bias.reshape(width // EMB, EMB), placement, owned_ids,
    )
    return pl.pallas_call(
        copy_body,
        out_shape=shapes,
        in_specs=[vmem, vmem],
        out_specs=(hbm, hbm),
        scratch_shapes=[pltpu.SemaphoreType.DMA((2,))],
        name="hand_over",
    )(*[pltpu.with_memory_space_constraint(s, pltpu.VMEM) for s in sums])


def solution(mesh):
    in_specs = (
        P(("grp", "tbl"), None),
        P(("grp", "tbl"), None),
        P(),
        P(),
        P(),
        P(),
        P("tbl", None, "grp"),
    )
    out_specs = (P(("grp", "tbl"), None), P("tbl", "grp", None))
    fused = halving_fits(mesh.shape["grp"], mesh.shape["tbl"])
    return jax.shard_map(
        on_device_fused if fused else on_device, mesh=mesh, in_specs=in_specs, out_specs=out_specs, check_vma=False
    )
```

time: 50.6 us -> 43.8 us (0.87)
  Pallas kernels: 49.7 us -> 42.9 us
    pallas_call x1, Pallas kernels: 47.9 us -> 42.2 us  [on_device_fused(): pl.pallas_call(functools.partial(fused_body, n_grp, n_tbl, scale, plan, t...]
    pallas_call x1, Pallas kernels: 1.78 us -> 0.76 us  [on_device_fused(): pl.pallas_call(copy_body, out_shape=shapes, in_specs=[vmem, vmem], out_sp...]
where the time goes in v1:
time: 43.8 us; the launch traced here: 43.6 us
  Pallas kernels  42.9 us (98%)
  between operations  0.64 us (1%)
    pallas_call x1, Pallas kernels, on_device_fused(): pl.pallas_call(functools.partial(fused_body, n_grp, n_tbl, scale, plan, t...  42.2 us

profile of v1, /device:TPU:0, one launch (start us, length us, event | category | flops | bytes accessed | tf_op | source)
XLA Modules:
  0.0 43.6 jit_solution(5523221704788960703)
XLA Ops:
  0.6 42.2 %cross_backward.1 = (f32[8,6912]{1,0:T(8,128)S(1)}, f32[5,64,128]{2,1,0:T(8,128)S(1)}) custom-call(bf16[128,3456]{1,0:T(8,128)(2,1)} %refs_0_.1, bf16[128,3456]{1,0:T(8,128)(2,1)} %refs_1_.1, bf16[256,3456]{1,0:T(8,128)(2,1)} %refs_2_.1, bf16[256,3456]{1,0:T(8,128)(2,1)} %refs_3_.1, f32[27,128]{1,0:T(8,128)} %bitcast.1, s32[26]{0:T(128)} %refs_5_.1, ...), custom_call_target="tpu_custom_call" | custom-call | tf_op jit(solution)/shard_map/cross_backward/pallas_call | solution.py:515
  42.8 0.8 %hand_over.1 = (f32[8,6912]{1,0:T(8,128)}, f32[5,64,128]{2,1,0:T(8,128)}) custom-call(f32[8,6912]{1,0:T(8,128)S(1)} %get-tuple-element.4.cross_ref, f32[5,64,128]{2,1,0:T(8,128)S(1)} %get-tuple-element.5.table_ref), custom_call_target="tpu_custom_call" | custom-call | tf_op jit(solution)/shard_map/hand_over/pallas_call | solution.py:529

commit v2 on v1

--- a/solution.py
+++ b/solution.py
@@ -450,7 +450,7 @@
                 dst[pair + (i % slots_dev,)] = (value * there).astype(kind)
                 return carry
 
-            lax.fori_loop(0, slots_dev * n_tbl // 2, run, 0, unroll=5)
+            lax.fori_loop(0, slots_dev * n_tbl // 2, run, 0, unroll=True)
 
         bit = bits[dims[1]]
         each_slot(1 - bit, r["s%s1" % name], bf16)

time: 43.8 us -> 42.9 us (0.979)
  Pallas kernels: 42.9 us -> 42 us
    pallas_call x1, Pallas kernels: 42.2 us -> 41.3 us  [on_device_fused(): pl.pallas_call(functools.partial(fused_body, n_grp, n_tbl, scale, plan, t...]
where the time goes in v2:
time: 42.9 us; the launch traced here: 42.7 us
  Pallas kernels  42 us (98%)
  between operations  0.64 us (1%)
    pallas_call x1, Pallas kernels, on_device_fused(): pl.pallas_call(functools.partial(fused_body, n_grp, n_tbl, scale, plan, t...  41.3 us

profile of v2, /device:TPU:0, one launch (start us, length us, event | category | flops | bytes accessed | tf_op | source)
XLA Modules:
  0.0 42.7 jit_solution(13978763492752309393)
XLA Ops:
  0.6 41.3 %cross_backward.1 = (f32[8,6912]{1,0:T(8,128)S(1)}, f32[5,64,128]{2,1,0:T(8,128)S(1)}) custom-call(bf16[128,3456]{1,0:T(8,128)(2,1)} %refs_0_.1, bf16[128,3456]{1,0:T(8,128)(2,1)} %refs_1_.1, bf16[256,3456]{1,0:T(8,128)(2,1)} %refs_2_.1, bf16[256,3456]{1,0:T(8,128)(2,1)} %refs_3_.1, f32[27,128]{1,0:T(8,128)} %bitcast.1, s32[26]{0:T(128)} %refs_5_.1, ...), custom_call_target="tpu_custom_call" | custom-call | tf_op jit(solution)/shard_map/cross_backward/pallas_call | solution.py:515
  41.9 0.8 %hand_over.1 = (f32[8,6912]{1,0:T(8,128)}, f32[5,64,128]{2,1,0:T(8,128)}) custom-call(f32[8,6912]{1,0:T(8,128)S(1)} %get-tuple-element.4.cross_ref, f32[5,64,128]{2,1,0:T(8,128)S(1)} %get-tuple-element.5.table_ref), custom_call_target="tpu_custom_call" | custom-call | tf_op jit(solution)/shard_map/hand_over/pallas_call | solution.py:529
